TPU v7x, 256 devices: a whole 4x4x8 slice. The times are simulated.
256 devices in a mesh: ctx: 8 (over z_hi, core), exp: 32 (over x, z_lo, y).
Axes of the slice: x: 4, y: 4, z: 8 (z_hi: 4, z_lo: 2; z = z_hi * 2 + z_lo), core: 2. Of those that a mesh axis runs over, the one named last changes fastest.
Arguments:
- queries: bfloat16 [4096, 4096], P('ctx', 'exp'), may hold values from -8 to 8
- doc_keys: bfloat16 [8192, 4096], P('ctx', 'exp'), may hold values from -8 to 8
- doc_values: bfloat16 [8192, 4096], P('ctx', 'exp'), may hold values from -6 to 6
- residual: bfloat16 [4096, 4096], P(('ctx', 'exp')), may hold values from -3 to 3
- out_weight: bfloat16 [4096, 4096], P('exp'), may hold values from -0.09375 to 0.09375
- norm_gain: float32 [4096], replicated, may hold values from 0.1 to 1.9
- expert_ids: int32 [4096, 1], P(('ctx', 'exp')), may hold values from 0 to 7; in each aligned block of 16 rows (0 to 15, 16 to 31, ...) at most 4 rows name the same one
- gate_up: bfloat16 [32, 4096, 5120], P('exp', None, 'ctx'), may hold values from -0.09375 to 0.09375
- down_weight: bfloat16 [32, 2560, 4096], P('exp', 'ctx'), may hold values from -0.0625 to 0.0625
Outputs:
- attended: bfloat16 [4096, 4096], P(('ctx', 'exp'))
- expert_out: bfloat16 [4096, 4096], P(('ctx', 'exp'))
Inputs may be any that keep to these rules, and one draw needn't show every extreme that they name: `expert_ids`: in each aligned block of 16 tokens, the rows of one device, no expert is named more than 4 times.
All inputs are finite; a program needn't handle non-finite values.
Results may differ from a plain program's by a relative error of at most 0.033.
Values may be sent and summed in bfloat16 or wider, within the bound.
No kernel may reach another device: no remote copies, remote signals or barrier semaphores. Data moves between devices by JAX's collectives and lax.ppermute only.
A program may use at most 128 MiB of HBM per device.

v0:
```python
import jax
import jax.numpy as jnp
from jax import lax
from jax.sharding import PartitionSpec as P

DH = 64
QUARTERS = 4


def score_rows(query_rows, key_rows, head_count):
    query_split = query_rows.reshape(query_rows.shape[0], head_count, -1)
    key_split = key_rows.reshape(key_rows.shape[0], head_count, -1)
    factor = query_split.shape[2] ** (-0.5)
    return (
        jnp.einsum("qhd,khd->qhk", query_split, key_split, preferred_element_type=jnp.float32)
        * factor
    )


def weigh_rows(weights, value_rows, head_count):
    value_split = value_rows.reshape(value_rows.shape[0], head_count, -1)
    return jnp.einsum(
        "qhk,khd->qhd",
        weights.astype(jnp.bfloat16),
        value_split,
        preferred_element_type=jnp.float32,
    )


def on_device(
    queries, doc_keys, doc_values, residual, out_weight, norm_gain, expert_ids, gate_up, down_weight
):
    head_count = queries.shape[1] // DH
    query_count = queries.shape[0]
    row_top = jnp.full((query_count, head_count), -jnp.inf, jnp.float32)
    row_total = jnp.zeros((query_count, head_count), jnp.float32)
    weighted = jnp.zeros((query_count, head_count, DH), jnp.float32)
    scores = score_rows(queries, lax.all_gather(doc_keys, "ctx", axis=0, tiled=True), head_count)
    new_top = jnp.max(scores, axis=2)
    decay_now = jnp.exp(row_top - new_top)
    weights = jnp.exp(scores - new_top[:, :, None])
    row_total = row_total * decay_now + jnp.sum(weights, axis=2)
    weighted = weighted * decay_now[:, :, None] + weigh_rows(
        weights, lax.all_gather(doc_values, "ctx", axis=0, tiled=True), head_count
    )
    row_top, row_total, weighted = (new_top, row_total, weighted)
    context = (
        (weighted / row_total[:, :, None])
        .reshape(query_count, head_count * DH)
        .astype(jnp.bfloat16)
    )
    row_count = residual.shape[0]
    mixed_heads = lax.psum_scatter(
        jnp.dot(context, out_weight, preferred_element_type=jnp.float32).astype(jnp.bfloat16),
        "exp",
        scatter_dimension=0,
        tiled=True,
    ).astype(jnp.float32)
    attended = lax.optimization_barrier(
        (residual.astype(jnp.float32) + mixed_heads).astype(jnp.bfloat16)
    )
    widened = attended.astype(jnp.float32)
    normed = (
        widened * lax.rsqrt(jnp.mean(widened * widened, axis=1, keepdims=True) + 1e-06) * norm_gain
    ).astype(jnp.bfloat16)
    routes = expert_ids[:, 0]
    positions = jnp.arange(row_count, dtype=jnp.int32)
    earlier = (routes[:, None] == routes[None, :]) & (positions[:, None] > positions[None, :])
    slot_rank = jnp.sum(earlier.astype(jnp.int32), axis=1)
    targets = lax.axis_size("exp")
    held_experts = targets // QUARTERS
    capacity = 2 * row_count // held_experts
    target_expert = jnp.arange(targets, dtype=jnp.int32) // QUARTERS
    slot_range = jnp.arange(capacity, dtype=jnp.int32)
    chosen = (routes[None, None, :] == target_expert[:, None, None]) & (
        slot_rank[None, None, :] == slot_range[None, :, None]
    )
    outgoing = jnp.einsum(
        "ekt,td->ekd", chosen.astype(jnp.bfloat16), normed, preferred_element_type=jnp.float32
    ).astype(jnp.bfloat16)
    incoming = lax.all_to_all(outgoing, "exp", split_axis=0, concat_axis=0, tiled=True)
    stacked = incoming.reshape(targets * capacity, incoming.shape[2])
    slice_width = down_weight.shape[1]
    gate_and_up = jnp.dot(
        lax.all_gather(stacked, "ctx", axis=0, tiled=True),
        gate_up[0],
        preferred_element_type=jnp.float32,
    )
    hidden = (jax.nn.silu(gate_and_up[:, :slice_width]) * gate_and_up[:, slice_width:]).astype(
        jnp.bfloat16
    )
    quarter_sums = lax.psum_scatter(
        jnp.dot(hidden, down_weight[0], preferred_element_type=jnp.float32).astype(jnp.bfloat16),
        "ctx",
        scatter_dimension=0,
        tiled=True,
    ).astype(jnp.float32)
    returned = lax.all_to_all(
        quarter_sums.reshape(targets, capacity, -1).astype(jnp.bfloat16),
        "exp",
        split_axis=0,
        concat_axis=0,
        tiled=True,
    ).astype(jnp.float32)
    senders = routes[:, None] * QUARTERS + jnp.arange(QUARTERS, dtype=jnp.int32)[None, :]
    expert_sum = jnp.sum(returned[senders, slot_rank[:, None]], axis=1)
    return (attended, expert_sum.astype(jnp.bfloat16))


def solution(mesh):
    return jax.shard_map(
        on_device,
        mesh=mesh,
        in_specs=(
            P("ctx", "exp"),
            P("ctx", "exp"),
            P("ctx", "exp"),
            P(("ctx", "exp"), None),
            P("exp", None),
            P(),
            P(("ctx", "exp"), None),
            P("exp", None, "ctx"),
            P("exp", "ctx", None),
        ),
        out_specs=(P(("ctx", "exp"), None), P(("ctx", "exp"), None)),
        check_vma=False,
    )
```

profile of v0, /device:TPU:8, one launch (start us, length us, event | category | flops | bytes accessed | tf_op | source)
XLA Modules:
  0.0 540.4 jit_solution(8661302534526715291)
XLA Ops:
  7.2 0.0 copy-start
  7.2 0.0 all-gather.4.cloned.1.call-start
  7.2 0.7 all-gather.4.cloned.1.call-update
  7.9 0.0 all-gather.6.cloned.1.call-start
  8.0 0.7 all-gather.6.cloned.1.call-update
  8.7 0.0 reduce-scatter.3.cloned.1.call-start
  8.7 1.0 copy.26
  9.7 39.3 %all-gather.4.cloned.1.call-done = bf16[8192,128]{1,0:T(8,128)(2,1)} async-done(((bf16[1024,128]{1,0:T(8,128)(2,1)}), bf16[8192,128]{1,0:T(8,128)(2,1)}) %all-gather.4.cloned.1.call-update) | async-done | bytes 2097168 | tf_op jit(solution)/shard_map/all_gather | solution.py:38
  49.0 4.1 copy.25
  53.1 15.2 %bitcast_reduce_fusion = (f32[512,2]{0,1:T(2,128)S(1)}, f32[2,8192,512]{2,1,0:T(8,128)}) fusion(bf16[8192,2,64]{0,2,1:T(8,128)(2,1)} %bitcast.51, bf16[512,2,64]{0,2,1:T(8,128)(2,1)S(1)} %bitcast.53), kind=kOutput, calls=%fused_computation.2 | convolution fusion | flops 1090518016 | bytes 35786752 | tf_op jit(solution)/shard_map/qhd,khd->qhk/dot_general | solution.py:15
  68.4 15.3 %fusion.1 = f32[512,2]{0,1:T(2,128)S(1)} fusion(f32[2,8192,512]{2,1,0:T(8,128)} %get-tuple-element.5, f32[512,2]{0,1:T(2,128)S(1)} %get-tuple-element.4), kind=kLoop, calls=%fused_computation.4 | loop fusion | flops 25164800 | bytes 33562624 | tf_op jit(solution)/shard_map/reduce_sum | solution.py:42
  83.7 1.8 all-gather.6.cloned.1.call-done
  85.4 4.1 copy.27
  89.6 0.0 copy-start.2
  89.6 14.1 %fusion.18 = bf16[512,2,64]{0,2,1:T(8,128)(2,1)S(1)} fusion(bf16[8192,2,64]{0,2,1:T(8,128)(2,1)} %bitcast.50, f32[2,8192,512]{2,1,0:T(8,128)} %get-tuple-element.5, f32[512,2]{0,1:T(2,128)S(1)} %get-tuple-element.4, f32[512,2]{0,1:T(2,128)S(1)} %get-tuple-element.3, f32[512,2]{0,1:T(2,128)S(1)} %get-tuple-element.2), kind=kOutput, calls=%fused_computation.18 | convolution fusion | flops 1099104256 | bytes 35794944 | tf_op jit(solution)/shard_map/qhk,khd->qhd/dot_general | solution.py:22
  103.7 0.0 copy-done.2
  103.7 0.0 copy-start.5
  103.7 0.0 copy-start.3
  103.7 3.2 convolution_convert_fusion.1
  106.9 0.0 copy-start.4
  106.9 0.0 reduce-scatter.3.cloned.1.call-update
  106.9 0.0 all-gather.8.cloned.1.call-start
  107.0 0.0 copy-done.5
  107.0 0.2 convert_reduce_fusion
  107.2 0.1 broadcast_compare_fusion
  107.3 166.1 %reduce-scatter.3.cloned.1.call-done = bf16[16,4096]{1,0:T(8,128)(2,1)} async-done(((bf16[512,4096]{1,0:T(8,128)(2,1)}), bf16[16,4096]{1,0:T(8,128)(2,1)}) %reduce-scatter.3.cloned.1.call-update) | async-done | bytes 131088 | tf_op jit(solution)/shard_map/reduce_scatter | solution.py:53
  273.4 0.0 copy-done.3
  273.4 0.9 add_convert_fusion
  274.3 0.0 copy-start.1
  274.3 0.1 fusion.23
  274.5 0.0 copy-done.4
  274.5 0.6 convolution_convert_fusion.2
  275.0 0.8 copy.29
  275.9 21.7 %all_to_all.10 = bf16[32,4,4096]{2,1,0:T(4,128)(2,1)} all-to-all(bf16[32,4,4096]{2,1,0:T(4,128)(2,1)S(1)} %copy.29), channel_id=1, replica_groups=mesh['ctx'=8,'exp'=32] {'exp'}, dimensions={0} | all-to-all | bytes 2097152 | tf_op jit(solution)/shard_map/all_to_all | solution.py:81
  297.6 2.2 reshape.167
  299.8 0.0 all-gather.8.cloned.1.call-update
  299.8 0.0 copy-done.1
  299.8 0.2 reduce-scatter.5.cloned.1.call-start
  300.0 80.6 %all-gather.8.cloned.1.call-done = bf16[1024,4096]{1,0:T(8,128)(2,1)} async-done(((bf16[128,4096]{1,0:T(8,128)(2,1)}), bf16[1024,4096]{1,0:T(8,128)(2,1)}) %all-gather.8.cloned.1.call-update) | async-done | bytes 8388624 | tf_op jit(solution)/shard_map/all_gather | solution.py:85
  380.6 9.6 %fusion.5 = f32[1024,640]{0,1:T(8,128)S(1)} fusion(bf16[1024,4096]{1,0:T(8,128)(2,1)} %all-gather.8.cloned.1.call-done, bf16[1,4096,640]{2,1,0:T(8,128)(2,1)} %param.16), kind=kOutput, calls=%fused_computation.9 | convolution fusion | flops 5368709120 | bytes 16252928 | tf_op jit(solution)/shard_map/dot_general | solution.py:84
  390.3 0.0 copy-done
  390.3 7.0 %convolution_convert_fusion = bf16[1024,4096]{1,0:T(8,128)(2,1)} fusion(bf16[1,320,4096]{2,1,0:T(8,128)(2,1)S(1)} %copy-done, f32[1024,640]{0,1:T(8,128)S(1)} %fusion.5), kind=kOutput, calls=%fused_computation.7 | convolution fusion | flops 2690514944 | bytes 13631488 | tf_op jit(solution)/shard_map/dot_general | solution.py:93
  397.2 0.0 reduce-scatter.5.cloned.1.call-update
  397.3 100.7 %reduce-scatter.5.cloned.1.call-done = bf16[128,4096]{1,0:T(8,128)(2,1)} async-done(((bf16[1024,4096]{1,0:T(8,128)(2,1)}), bf16[128,4096]{1,0:T(8,128)(2,1)}) %reduce-scatter.5.cloned.1.call-update) | async-done | bytes 1048592 | tf_op jit(solution)/shard_map/reduce_scatter | solution.py:92
  497.9 2.2 convert_element_type.64
  500.1 9.8 %all-to-all-start.1 = ((bf16[32,4,4096]{2,1,0:T(4,128)(2,1)}), bf16[32,4,4096]{2,1,0:T(4,128)(2,1)}, u32[]{:S(2)}, u32[]{:S(2)}) async-start(bf16[32,4,4096]{2,1,0:T(4,128)(2,1)} %convert_element_type.64), calls=%async_computation.3 | async-start | bytes 2097152 | tf_op jit(solution)/shard_map/all_to_all | solution.py:98
  509.9 0.1 fusion.35
  510.0 0.1 reshape.168
  510.1 12.5 %all-to-all-done.1 = bf16[32,4,4096]{2,1,0:T(4,128)(2,1)} async-done(((bf16[32,4,4096]{2,1,0:T(4,128)(2,1)}), bf16[32,4,4096]{2,1,0:T(4,128)(2,1)}, u32[]{:S(2)}, u32[]{:S(2)}) %all-to-all-start.1) | async-done | bytes 1048608 | tf_op jit(solution)/shard_map/all_to_all | solution.py:98
  522.6 2.8 convert_element_type.65
  525.4 3.4 gather_fusion
  528.9 2.5 reshape.171
  531.4 2.5 reduce_sum.39
  (6 shorter events, 0.0 us)
Async XLA Ops:
  7.2 383.1 %copy-start = (bf16[1,320,4096]{2,1,0:T(8,128)(2,1)S(1)}, bf16[1,320,4096]{2,1,0:T(8,128)(2,1)}, u32[]{:S(2)}) copy-start(bf16[1,320,4096]{2,1,0:T(8,128)(2,1)} %param.17) | copy-start | bytes 7864324
  7.2 41.8 %all-gather.4.cloned.1.call-start = ((), (), s32[]{:S(2)}) async-start(), calls=%async_computation.4 | async-start | bytes 2359296 | tf_op jit(solution)/shard_map/all_gather | solution.py:38
  7.9 77.5 %all-gather.6.cloned.1.call-start = ((), (), s32[]{:S(2)}) async-start(), calls=%async_computation.5 | async-start | bytes 2359296 | tf_op jit(solution)/shard_map/all_gather | solution.py:44
  8.7 264.7 %reduce-scatter.3.cloned.1.call-start = ((), (), s32[]{:S(2)}) async-start(), calls=%async_computation.6 | async-start | bytes 4325376 | tf_op jit(solution)/shard_map/reduce_scatter | solution.py:53
  89.6 14.1 %copy-start.2 = (bf16[128,4096]{1,0:T(8,128)(2,1)S(1)}, bf16[128,4096]{1,0:T(8,128)(2,1)}, u32[]{:S(2)}) copy-start(bf16[128,4096]{1,0:T(8,128)(2,1)} %param.13) | copy-start | bytes 3145732
  103.7 3.3 copy-start.5
  103.7 169.7 %copy-start.3 = (bf16[16,4096]{1,0:T(8,128)(2,1)S(1)}, bf16[16,4096]{1,0:T(8,128)(2,1)}, u32[]{:S(2)}) copy-start(bf16[16,4096]{1,0:T(8,128)(2,1)} %param.12) | copy-start | bytes 393220
  106.9 167.6 %copy-start.4 = (f32[4096]{0:T(1024)S(1)}, f32[4096]{0:T(1024)}, u32[]{:S(2)}) copy-start(f32[4096]{0:T(1024)} %param.14) | copy-start | bytes 49156
  106.9 273.7 %all-gather.8.cloned.1.call-start = ((), (), s32[]{:S(2)}) async-start(), calls=%async_computation.7 | async-start | bytes 9437184 | tf_op jit(solution)/shard_map/all_gather | solution.py:85
  274.3 25.5 %copy-start.1 = (bf16[16,4096]{1,0:T(8,128)(2,1)}, bf16[16,4096]{1,0:T(8,128)(2,1)S(1)}, u32[]{:S(2)}) copy-start(bf16[16,4096]{1,0:T(8,128)(2,1)S(1)} %add_convert_fusion) | copy-start | bytes 393220
  299.8 198.1 %reduce-scatter.5.cloned.1.call-start = ((), (), s32[]{:S(2)}) async-start(), calls=%async_computation.8 | async-start | bytes 9437184 | tf_op jit(solution)/shard_map/reduce_scatter | solution.py:92
  500.1 22.5 %all-to-all-start.1 = ((bf16[32,4,4096]{2,1,0:T(4,128)(2,1)}), bf16[32,4,4096]{2,1,0:T(4,128)(2,1)}, u32[]{:S(2)}, u32[]{:S(2)}) async-start(bf16[32,4,4096]{2,1,0:T(4,128)(2,1)} %convert_element_type.64), calls=%async_computation.3 | async-start | bytes 2097152 | tf_op jit(solution)/shard_map/all_to_all | solution.py:98
Sparse Core Ops, SparseCore 0:
  9.8 39.0 all-gather.3
  50.8 34.5 all-gather.5
  107.1 166.2 reduce-scatter.2
  299.9 80.6 all-gather.7
  397.4 100.4 reduce-scatter.4
where the time goes:
time: 541 us; the launch traced here: 540 us
  waiting for transfers between devices  402 us (74%)
  matrix products  49.7 us (9%)
  other arithmetic  22.1 us (4%)
  blocking collectives  21.7 us (4%)
  local copies, waits for them, and re-layouts  20.6 us (4%)
  between operations  13.9 us (3%)
  starting transfers between devices  10.1 us (2%)
    reduce_scatter x1, waiting for transfers between devices, on_device(): lax.psum_scatter(jnp.dot(context, out_weight, preferred_element_type=jnp....  166 us
    reduce_scatter x1, waiting for transfers between devices, on_device(): lax.psum_scatter(jnp.dot(hidden, down_weight[0], preferred_element_type=j...  101 us
    all_gather x1, waiting for transfers between devices, on_device(): lax.all_gather(stacked, 'ctx', axis=0, tiled=True)  80.6 us
    all_gather x1, waiting for transfers between devices, on_device(): lax.all_gather(doc_keys, 'ctx', axis=0, tiled=True)  39.3 us
    all_to_all x1, blocking collectives, on_device(): lax.all_to_all(outgoing, 'exp', split_axis=0, concat_axis=0, tiled=True)  21.7 us
    reduce_sum x1, other arithmetic, on_device(): row_total = row_total * decay_now + jnp.sum(weights, axis=2)  15.3 us
    dot_general x1, matrix products, score_rows(): jnp.einsum('qhd,khd->qhk', query_split, key_split, preferred_element_type...  15.2 us
    dot_general x1, matrix products, weigh_rows(): jnp.einsum('qhk,khd->qhd', weights.astype(jnp.bfloat16), value_split, pre...  14.1 us
  transfers between devices with their start and end apart: 6, of which 6 were waited for; matrix products, arithmetic and copies ran while one was open for 7% of the time, Pallas kernels for 0%

commit v1 on v0

--- a/solution.py
+++ b/solution.py
@@ -5,6 +5,13 @@
 
 DH = 64
 QUARTERS = 4
+
+
+def swapped_in(shard, name, dim):
+    n_dev = lax.axis_size(name)
+    tiles = jnp.stack([shard for _ in range(n_dev)])
+    tiles = lax.all_to_all(tiles, name, split_axis=0, concat_axis=0)
+    return jnp.concatenate(tiles, axis=dim)
 
 
 def score_rows(query_rows, key_rows, head_count):
@@ -82,9 +89,7 @@
     stacked = incoming.reshape(targets * capacity, incoming.shape[2])
     slice_width = down_weight.shape[1]
     gate_and_up = jnp.dot(
-        lax.all_gather(stacked, "ctx", axis=0, tiled=True),
-        gate_up[0],
-        preferred_element_type=jnp.float32,
+        swapped_in(stacked, "ctx", 0), gate_up[0], preferred_element_type=jnp.float32
     )
     hidden = (jax.nn.silu(gate_and_up[:, :slice_width]) * gate_and_up[:, slice_width:]).astype(
         jnp.bfloat16

time: 541 us -> 645 us (1.19)
  blocking collectives: 21.7 us -> 213 us
  waiting for transfers between devices: 402 us -> 314 us
    all_to_all x0 -> x1, blocking collectives: none -> 192 us  [swapped_in(): tiles = lax.all_to_all(tiles, name, split_axis=0, concat_axis=0)]
    all_gather x1 -> x0, waiting for transfers between devices: 80.6 us -> none  [on_device(): lax.all_gather(stacked, 'ctx', axis=0, tiled=True)]
    reduce_scatter x1, waiting for transfers between devices: 101 us -> 92.1 us  [on_device(): lax.psum_scatter(jnp.dot(hidden, down_weight[0], preferred_element_type=j...]
  transfers between devices with their start and end apart: 6 -> 5, of which waited for: 6 -> 5; matrix products, arithmetic and copies ran while one was open for 7% -> 6% of each run, Pallas kernels for 0% -> 0%
where the time goes in v1:
time: 645 us; the launch traced here: 644 us
  waiting for transfers between devices  314 us (49%)
  blocking collectives  213 us (33%)
  matrix products  48.3 us (7%)
  local copies, waits for them, and re-layouts  23.3 us (4%)
  other arithmetic  22.1 us (3%)
  between operations  13.9 us (2%)
  starting transfers between devices  9.68 us (2%)
    all_to_all x1, blocking collectives, swapped_in(): tiles = lax.all_to_all(tiles, name, split_axis=0, concat_axis=0)  192 us
    reduce_scatter x1, waiting for transfers between devices, on_device(): lax.psum_scatter(jnp.dot(context, out_weight, preferred_element_type=jnp....  167 us
    reduce_scatter x1, waiting for transfers between devices, on_device(): lax.psum_scatter(jnp.dot(hidden, down_weight[0], preferred_element_type=j...  92.1 us
    all_gather x1, waiting for transfers between devices, on_device(): lax.all_gather(doc_keys, 'ctx', axis=0, tiled=True)  39.3 us
    all_to_all x1, blocking collectives, on_device(): lax.all_to_all(outgoing, 'exp', split_axis=0, concat_axis=0, tiled=True)  21.1 us
    reduce_sum x1, other arithmetic, on_device(): row_total = row_total * decay_now + jnp.sum(weights, axis=2)  15.3 us
    dot_general x1, matrix products, score_rows(): jnp.einsum('qhd,khd->qhk', query_split, key_split, preferred_element_type...  15.2 us
    dot_general x1, matrix products, weigh_rows(): jnp.einsum('qhk,khd->qhd', weights.astype(jnp.bfloat16), value_split, pre...  14.1 us
  transfers between devices with their start and end apart: 5, of which 5 were waited for; matrix products, arithmetic and copies ran while one was open for 6% of the time, Pallas kernels for 0%

profile of v1, /device:TPU:8, one launch (start us, length us, event | category | flops | bytes accessed | tf_op | source)
XLA Modules:
  0.0 644.0 jit_solution(14036507229472581113)
XLA Ops:
  7.2 0.0 copy-start
  7.2 0.0 all-gather.3.cloned.1.call-start
  7.2 0.7 all-gather.3.cloned.1.call-update
  7.9 0.0 all-gather.5.cloned.1.call-start
  8.0 0.7 all-gather.5.cloned.1.call-update
  8.7 0.0 reduce-scatter.3.cloned.1.call-start
  8.7 1.0 copy.26
  9.7 39.3 %all-gather.3.cloned.1.call-done = bf16[8192,128]{1,0:T(8,128)(2,1)} async-done(((bf16[1024,128]{1,0:T(8,128)(2,1)}), bf16[8192,128]{1,0:T(8,128)(2,1)}) %all-gather.3.cloned.1.call-update) | async-done | bytes 2097168 | tf_op jit(solution)/shard_map/all_gather | solution.py:45
  49.0 4.1 copy.25
  53.1 15.2 %bitcast_reduce_fusion = (f32[512,2]{0,1:T(2,128)S(1)}, f32[2,8192,512]{2,1,0:T(8,128)}) fusion(bf16[8192,2,64]{0,2,1:T(8,128)(2,1)} %bitcast.52, bf16[512,2,64]{0,2,1:T(8,128)(2,1)S(1)} %bitcast.55), kind=kOutput, calls=%fused_computation.2 | convolution fusion | flops 1090518016 | bytes 35786752 | tf_op jit(solution)/shard_map/qhd,khd->qhk/dot_general | solution.py:22
  68.3 15.3 %fusion.1 = f32[512,2]{0,1:T(2,128)S(1)} fusion(f32[2,8192,512]{2,1,0:T(8,128)} %get-tuple-element.5, f32[512,2]{0,1:T(2,128)S(1)} %get-tuple-element.4), kind=kLoop, calls=%fused_computation.4 | loop fusion | flops 25164800 | bytes 33562624 | tf_op jit(solution)/shard_map/reduce_sum | solution.py:49
  83.6 1.8 all-gather.5.cloned.1.call-done
  85.4 4.1 copy.27
  89.5 0.0 copy-start.2
  89.5 14.1 %fusion.18 = bf16[512,2,64]{0,2,1:T(8,128)(2,1)S(1)} fusion(bf16[8192,2,64]{0,2,1:T(8,128)(2,1)} %bitcast.51, f32[2,8192,512]{2,1,0:T(8,128)} %get-tuple-element.5, f32[512,2]{0,1:T(2,128)S(1)} %get-tuple-element.4, f32[512,2]{0,1:T(2,128)S(1)} %get-tuple-element.3, f32[512,2]{0,1:T(2,128)S(1)} %get-tuple-element.2), kind=kOutput, calls=%fused_computation.18 | convolution fusion | flops 1099104256 | bytes 35794944 | tf_op jit(solution)/shard_map/qhk,khd->qhd/dot_general | solution.py:29
  103.6 0.0 copy-done.2
  103.6 0.0 copy-start.5
  103.6 0.0 copy-start.3
  103.7 0.0 copy-start.4
  103.7 3.2 convolution_convert_fusion.1
  106.9 0.0 reduce-scatter.3.cloned.1.call-update
  106.9 0.0 reduce-scatter.5.cloned.1.call-start
  107.0 0.0 copy-done.5
  107.0 0.2 convert_reduce_fusion
  107.2 0.1 broadcast_compare_fusion
  107.2 166.6 %reduce-scatter.3.cloned.1.call-done = bf16[16,4096]{1,0:T(8,128)(2,1)} async-done(((bf16[512,4096]{1,0:T(8,128)(2,1)}), bf16[16,4096]{1,0:T(8,128)(2,1)}) %reduce-scatter.3.cloned.1.call-update) | async-done | bytes 131088 | tf_op jit(solution)/shard_map/reduce_scatter | solution.py:60
  273.8 0.0 copy-done.3
  273.8 0.9 add_convert_fusion
  274.7 0.0 copy-start.1
  274.8 0.1 fusion.23
  274.9 0.5 copy-done.1
  275.4 0.0 copy-done.4
  275.4 0.5 convolution_convert_fusion.2
  276.0 0.8 copy.29
  276.8 21.1 %all_to_all.15 = bf16[32,4,4096]{2,1,0:T(4,128)(2,1)} all-to-all(bf16[32,4,4096]{2,1,0:T(4,128)(2,1)S(1)} %copy.29), channel_id=1, replica_groups=mesh['ctx'=8,'exp'=32] {'exp'}, dimensions={0} | all-to-all | bytes 2097152 | tf_op jit(solution)/shard_map/all_to_all | solution.py:88
  297.9 2.2 stack_reshape.2
  300.1 2.3 stack.3
  302.3 191.9 %all_to_all.16 = bf16[8,128,4096]{2,1,0:T(8,128)(2,1)S(1)} all-to-all(bf16[8,128,4096]{2,1,0:T(8,128)(2,1)S(1)} %stack.3), channel_id=1, replica_groups=mesh['ctx'=8,'exp'=32] {'ctx'}, dimensions={0} | all-to-all | bytes 16777216 | tf_op jit(solution)/shard_map/all_to_all | solution.py:13
  494.3 8.4 %fusion.5 = f32[1024,640]{0,1:T(8,128)S(1)} fusion(bf16[1024,4096]{1,0:T(8,128)(2,1)S(1)} %bitcast.53, bf16[1,4096,640]{2,1,0:T(8,128)(2,1)} %param.16), kind=kOutput, calls=%fused_computation.9 | convolution fusion | flops 5368709120 | bytes 16252928 | tf_op jit(solution)/shard_map/dot_general | solution.py:91
  502.6 0.0 copy-done
  502.6 6.9 %convolution_convert_fusion = bf16[1024,4096]{1,0:T(8,128)(2,1)} fusion(bf16[1,320,4096]{2,1,0:T(8,128)(2,1)S(1)} %copy-done, f32[1024,640]{0,1:T(8,128)S(1)} %fusion.5), kind=kOutput, calls=%fused_computation.7 | convolution fusion | flops 2690514944 | bytes 13631488 | tf_op jit(solution)/shard_map/dot_general | solution.py:98
  509.5 0.0 reduce-scatter.5.cloned.1.call-update
  509.6 92.1 %reduce-scatter.5.cloned.1.call-done = bf16[128,4096]{1,0:T(8,128)(2,1)} async-done(((bf16[1024,4096]{1,0:T(8,128)(2,1)}), bf16[128,4096]{1,0:T(8,128)(2,1)}) %reduce-scatter.5.cloned.1.call-update) | async-done | bytes 1048592 | tf_op jit(solution)/shard_map/reduce_scatter | solution.py:97
  601.6 2.2 convert_element_type.64
  603.9 9.5 %all-to-all-start.2 = ((bf16[32,4,4096]{2,1,0:T(4,128)(2,1)}), bf16[32,4,4096]{2,1,0:T(4,128)(2,1)}, u32[]{:S(2)}, u32[]{:S(2)}) async-start(bf16[32,4,4096]{2,1,0:T(4,128)(2,1)} %convert_element_type.64), calls=%async_computation.4 | async-start | bytes 2097152 | tf_op jit(solution)/shard_map/all_to_all | solution.py:103
  613.4 0.1 fusion.35
  613.5 0.1 reshape.170
  613.6 12.6 %all-to-all-done.2 = bf16[32,4,4096]{2,1,0:T(4,128)(2,1)} async-done(((bf16[32,4,4096]{2,1,0:T(4,128)(2,1)}), bf16[32,4,4096]{2,1,0:T(4,128)(2,1)}, u32[]{:S(2)}, u32[]{:S(2)}) %all-to-all-start.2) | async-done | bytes 1048608 | tf_op jit(solution)/shard_map/all_to_all | solution.py:103
  626.2 2.8 convert_element_type.65
  629.0 3.4 gather_fusion
  632.4 2.5 reshape.173
  634.9 2.5 reduce_sum.39
  (6 shorter events, 0.0 us)
Async XLA Ops:
  7.2 495.5 %copy-start = (bf16[1,320,4096]{2,1,0:T(8,128)(2,1)S(1)}, bf16[1,320,4096]{2,1,0:T(8,128)(2,1)}, u32[]{:S(2)}) copy-start(bf16[1,320,4096]{2,1,0:T(8,128)(2,1)} %param.17) | copy-start | bytes 7864324
  7.2 41.8 %all-gather.3.cloned.1.call-start = ((), (), s32[]{:S(2)}) async-start(), calls=%async_computation.5 | async-start | bytes 2359296 | tf_op jit(solution)/shard_map/all_gather | solution.py:45
  7.9 77.5 %all-gather.5.cloned.1.call-start = ((), (), s32[]{:S(2)}) async-start(), calls=%async_computation.6 | async-start | bytes 2359296 | tf_op jit(solution)/shard_map/all_gather | solution.py:51
  8.7 265.1 %reduce-scatter.3.cloned.1.call-start = ((), (), s32[]{:S(2)}) async-start(), calls=%async_computation.7 | async-start | bytes 4325376 | tf_op jit(solution)/shard_map/reduce_scatter | solution.py:60
  89.5 14.1 %copy-start.2 = (bf16[128,4096]{1,0:T(8,128)(2,1)S(1)}, bf16[128,4096]{1,0:T(8,128)(2,1)}, u32[]{:S(2)}) copy-start(bf16[128,4096]{1,0:T(8,128)(2,1)} %param.13) | copy-start | bytes 3145732
  103.6 3.3 copy-start.5
  103.6 170.2 %copy-start.3 = (bf16[16,4096]{1,0:T(8,128)(2,1)S(1)}, bf16[16,4096]{1,0:T(8,128)(2,1)}, u32[]{:S(2)}) copy-start(bf16[16,4096]{1,0:T(8,128)(2,1)} %param.12) | copy-start | bytes 393220
  103.7 171.7 %copy-start.4 = (f32[4096]{0:T(1024)S(1)}, f32[4096]{0:T(1024)}, u32[]{:S(2)}) copy-start(f32[4096]{0:T(1024)} %param.14) | copy-start | bytes 49156
  106.9 494.7 %reduce-scatter.5.cloned.1.call-start = ((), (), s32[]{:S(2)}) async-start(), calls=%async_computation.8 | async-start | bytes 9437184 | tf_op jit(solution)/shard_map/reduce_scatter | solution.py:97
  274.7 0.7 copy-start.1
  603.9 22.3 %all-to-all-start.2 = ((bf16[32,4,4096]{2,1,0:T(4,128)(2,1)}), bf16[32,4,4096]{2,1,0:T(4,128)(2,1)}, u32[]{:S(2)}, u32[]{:S(2)}) async-start(bf16[32,4,4096]{2,1,0:T(4,128)(2,1)} %convert_element_type.64), calls=%async_computation.4 | async-start | bytes 2097152 | tf_op jit(solution)/shard_map/all_to_all | solution.py:103
Sparse Core Ops, SparseCore 0:
  9.8 39.0 all-gather.2
  50.8 34.5 all-gather.4
  107.0 166.7 reduce-scatter.2
  509.7 91.9 reduce-scatter.4
